TPU v7x, 32 devices: a whole 2x2x4 slice. The times are simulated.
32 devices in a mesh: parts: 2 (over y), leaf: 16 (over z, x, core).
Axes of the slice: x: 2, y: 2, z: 4, core: 2. Of those that a mesh axis runs over, the one named last changes fastest.
Arguments:
- features: bfloat16 [32768, 512], P('leaf', 'parts'), parts along dimension 1, may hold values from -6 to 6
- vertex_order: int32 [16, 2048], P('leaf'), may hold values from 0 to 2047, each once within a row
- leaf_adjacency: int32 [16, 8, 3], P('leaf'), may hold values from 0 to 7
- near_blocks: bfloat16 [16, 8, 3, 256, 256], P('leaf'), may hold values from -0.21875 to 0.21875
- basis: bfloat16 [4, 32768, 256], P(None, 'leaf'), may hold values from -0.07432544 to 0.07432544
Outputs:
- smoothed: bfloat16 [32768, 512], P('leaf', 'parts'), parts along dimension 1
There are 2 independent parts, one for each index of `parts`. A program takes and returns all parts, laid end to end along the dimension named above; an argument that names none is the same for every part. Nothing has to cross between parts.
All inputs are finite; a program needn't handle non-finite values.
Results may differ from a plain program's by a relative error of at most 0.0048.
Values may be sent and summed in bfloat16 or wider, within the bound.
A program may use at most 64 MiB of HBM per device.

v0:
```python
import jax
import jax.numpy as jnp
from jax import lax
from jax.sharding import PartitionSpec as P


def from_partner(block, axis, bit):
    count = lax.axis_size(axis)
    route = []
    for low in range(count):
        high = low | 1 << bit
        if high != low and high < count:
            route += [(low, high), (high, low)]
    return lax.ppermute(block, axis, route)


def on_device(features, vertex_order, leaf_adjacency, near_blocks, basis):
    depth = lax.axis_size("leaf").bit_length() - 1
    leaf_rows = features.shape[0]
    columns = features.shape[1]
    sub_rows = near_blocks.shape[3]
    ordered = features[vertex_order[0]]
    pieces = ordered.reshape(leaf_rows // sub_rows, sub_rows, columns)
    chosen = pieces[leaf_adjacency[0]]
    near = jnp.einsum("snij,snjc->sic", near_blocks[0], chosen, preferred_element_type=jnp.float32)
    near = near.reshape(leaf_rows, columns)
    projection = jnp.einsum("bvr,vc->brc", basis, ordered, preferred_element_type=jnp.float32)
    finished = []
    for level in range(depth):
        running = projection[level]
        for bit in range(level):
            running = running + from_partner(running, "leaf", bit)
        finished.append(from_partner(running.astype(jnp.bfloat16), "leaf", level))
    sibling = jnp.stack(finished, axis=0)
    far = jnp.einsum("bvr,brc->vc", basis, sibling, preferred_element_type=jnp.float32)
    return (near + far).astype(jnp.bfloat16)


def solution(mesh):
    placed = (
        P("leaf", "parts"),
        P("leaf", None),
        P("leaf", None, None),
        P("leaf", None, None, None, None),
        P(None, "leaf", None),
    )
    return jax.shard_map(
        on_device, mesh=mesh, in_specs=placed, out_specs=P("leaf", "parts"), check_vma=False
    )
```

profile of v0, /device:TPU:0, one launch (start us, length us, event | category | flops | bytes accessed | tf_op | source)
XLA Modules:
  0.0 58.1 jit_solution(14578362678175814173)
XLA Ops:
  0.0 0.9 %compare_select_fusion = s32[2048,1]{0,1:T(1,128)S(1)} fusion(s32[1,2048]{1,0:T(1,128)} %param.6), kind=kLoop, calls=%fused_computation.24 | loop fusion | flops 6144 | bytes 16384 | tf_op jit(solution)/shard_map/select_n | solution.py:22
  0.9 9.9 %gather_fusion = bf16[2048,256]{1,0:T(8,128)(2,1)} fusion(bf16[2048,256]{1,0:T(8,128)(2,1)} %param.5, s32[2048]{0:T(1024)S(1)} %broadcast_clamp_fusion), kind=kCustom, calls=%fused_computation | custom fusion | bytes 2105344 | tf_op jit(solution)/shard_map/gather | solution.py:22
  10.8 3.8 %convolution_bitcast_fusion.1 = f32[4,256,256]{1,2,0:T(8,128)S(1)} fusion(bf16[4,2048,256]{2,1,0:T(8,128)(2,1)} %param.9, bf16[2048,256]{1,0:T(8,128)(2,1)} %gather_fusion), kind=kOutput, calls=%fused_computation.7 | convolution fusion | flops 1073741824 | bytes 6291456 | tf_op jit(solution)/shard_map/bvr,vc->brc/dot_general | solution.py:27
  14.7 0.5 collective-permute-start.1
  15.3 0.4 collective-permute-start.3
  15.7 0.7 %collective-permute-done.1 = f32[256,256]{0,1:T(8,128)S(1)} collective-permute-done((f32[256,256]{0,1:T(8,128)S(1)}, f32[256,256]{0,1:T(8,128)S(1)}, u32[]{:S(2)}, u32[]{:S(2)}) %collective-permute-start.1) | collective-permute-done | bytes 262176 | tf_op jit(solution)/shard_map/ppermute | solution.py:14
  16.4 0.4 collective-permute-done.6
  16.7 0.4 collective-permute-done.3
  17.1 0.8 %add_convert_fusion.2 = (bf16[256,256]{0,1:T(8,128)(2,1)S(1)}, f32[256,256]{0,1:T(8,128)S(1)}, f32[256,256]{0,1:T(8,128)}) fusion(f32[256,256]{0,1:T(8,128)S(1)} %collective-permute-done.1, f32[4,256,256]{1,2,0:T(8,128)S(1)} %convolution_bitcast_fusion.1, f32[256,256]{0,1:T(8,128)S(1)} %collective-permute-done.6, f32[256,256]{0,1:T(8,128)S(1)} %collective-permute-done.3), kind=kLoop, calls=%fused_computation.22 | loop fusion | flops 262144 | bytes 2228224 | tf_op jit(solution)/shard_map/convert_element_type | solution.py:33
  17.9 2.9 %collective-permute-start.7 = (f32[256,256]{0,1:T(8,128)S(1)}, f32[256,256]{0,1:T(8,128)}, u32[]{:S(2)}, u32[]{:S(2)}) collective-permute-start(f32[256,256]{0,1:T(8,128)S(1)} %get-tuple-element.6), channel_id=1, source_target_pairs={{0,2},{2,0},{1,3},{3,1},{4,6},{6,4},{5,7},{7,5},{8,10},{10,8},{9,1... | collective-permute-start | bytes 786440 | tf_op jit(solution)/shard_map/ppermute | solution.py:14
  20.8 0.7 %fusion.12 = bf16[256,256]{0,1:T(8,128)(2,1)} fusion(f32[4,256,256]{1,2,0:T(8,128)S(1)} %convolution_bitcast_fusion.1), kind=kLoop, calls=%fused_computation.23 | loop fusion | bytes 262144 | tf_op jit(solution)/shard_map/convert_element_type | solution.py:33
  21.8 6.2 %collective-permute-done.7 = f32[256,256]{0,1:T(8,128)} collective-permute-done((f32[256,256]{0,1:T(8,128)S(1)}, f32[256,256]{0,1:T(8,128)}, u32[]{:S(2)}, u32[]{:S(2)}) %collective-permute-start.7) | collective-permute-done | bytes 262176 | tf_op jit(solution)/shard_map/ppermute | solution.py:14
  28.0 1.7 %add.51 = f32[256,256]{0,1:T(8,128)} add(f32[256,256]{0,1:T(8,128)S(1)} %get-tuple-element.6, f32[256,256]{0,1:T(8,128)} %collective-permute-done.7) | non-fusion elementwise | flops 65536 | bytes 786432 | tf_op jit(solution)/shard_map/add | solution.py:32
  29.7 2.1 %collective-permute-start.8 = (f32[256,256]{0,1:T(8,128)}, f32[256,256]{0,1:T(8,128)S(1)}, u32[]{:S(2)}, u32[]{:S(2)}) collective-permute-start(f32[256,256]{0,1:T(8,128)} %add.51), channel_id=1, source_target_pairs={{0,4},{4,0},{1,5},{5,1},{2,6},{6,2},{3,7},{7,3},{8,12},{12,8},{9,1... | collective-permute-start | bytes 786440 | tf_op jit(solution)/shard_map/ppermute | solution.py:14
  31.8 3.7 %gather_fusion.1 = bf16[24,256,256]{2,1,0:T(8,128)(2,1)} fusion(bf16[8,256,256]{2,1,0:T(8,128)(2,1)} %bitcast.52, s32[1024]{0:T(1024)S(1)} %pad_clamp_fusion), kind=kCustom, calls=%fused_computation.1 | custom fusion | bytes 6291552 | tf_op jit(solution)/shard_map/gather | solution.py:24
  35.5 1.5 %collective-permute-start.2 = (bf16[256,256]{0,1:T(8,128)(2,1)S(1)}, bf16[256,256]{0,1:T(8,128)(2,1)}, u32[]{:S(2)}, u32[]{:S(2)}) collective-permute-start(bf16[256,256]{0,1:T(8,128)(2,1)S(1)} %get-tuple-element.5), channel_id=1, source_target_pairs={{0,2},{2,0},{1,3},{3,1},{4,6},{6,4},{5,7},{7,5},{8,10},{10,8},{9,1... | collective-permute-start | bytes 393224 | tf_op jit(solution)/shard_map/ppermute | solution.py:14
  37.0 1.7 %add_convert_fusion.1 = bf16[256,256]{0,1:T(8,128)(2,1)} fusion(f32[256,256]{0,1:T(8,128)} %get-tuple-element.7, f32[256,256]{0,1:T(8,128)} %collective-permute-done.4), kind=kLoop, calls=%fused_computation.21 | loop fusion | flops 131072 | bytes 655360 | tf_op jit(solution)/shard_map/convert_element_type | solution.py:33
  38.7 0.4 collective-permute-start.5
  39.2 1.6 %add_convert_fusion = bf16[256,256]{0,1:T(8,128)(2,1)} fusion(f32[256,256]{0,1:T(8,128)} %add.51, f32[256,256]{0,1:T(8,128)S(1)} %collective-permute-done.8), kind=kLoop, calls=%fused_computation.20 | loop fusion | flops 131072 | bytes 655360 | tf_op jit(solution)/shard_map/convert_element_type | solution.py:33
  40.8 2.6 %collective-permute-start.9 = (bf16[256,256]{0,1:T(8,128)(2,1)}, bf16[256,256]{0,1:T(8,128)(2,1)S(1)}, u32[]{:S(2)}, u32[]{:S(2)}) collective-permute-start(bf16[256,256]{0,1:T(8,128)(2,1)} %add_convert_fusion), channel_id=1, source_target_pairs={{0,8},{8,0},{1,9},{9,1},{2,10},{10,2},{3,11},{11,3},{4,12},{12,4},... | collective-permute-start | bytes 393224 | tf_op jit(solution)/shard_map/ppermute | solution.py:14
  43.4 4.2 %fusion = f32[8,256,256,1]{1,2,3,0:T(8,128)} fusion(bf16[8,3,256,256]{3,2,1,0:T(8,128)(2,1)} %bitcast.53, bf16[1,8,3,256,256]{4,3,2,1,0:T(8,128)(2,1)S(1)} %copy-done), kind=kOutput, calls=%fused_computation.2 | convolution fusion | flops 805306368 | bytes 8388608 | tf_op jit(solution)/shard_map/snij,snjc->sic/dot_general | solution.py:25
  47.6 2.9 %copy.12 = f32[2048,256]{0,1:T(8,128)} copy(f32[2048,256]{1,0:T(8,128)} %bitcast.54) | data formatting | bytes 4194304 | tf_op jit(solution)/shard_map/reshape | solution.py:26
  50.6 5.3 %fusion.3 = bf16[2048,256]{0,1:T(8,128)(2,1)} fusion(f32[2048,256]{0,1:T(8,128)} %copy.12, bf16[4,2048,256]{2,1,0:T(8,128)(2,1)} %param.9, bf16[1,256,256]{1,2,0:T(8,128)(2,1)S(1)} %bitcast.56, bf16[1,256,256]{1,2,0:T(8,128)(2,1)} %bitcast.17, bf16[1,256,256]{1,2,0:T(8,128)(2,1)} %bitcast.15, bf16[1,256,256]{1,2,0:T(8,128)(2,1)} %bitcast.13), kind=kOutput, calls=%fused_computation.6 | convolution fusion | flops 1075576832 | bytes 7864320 | tf_op jit(solution)/shard_map/bvr,brc->vc/dot_general | solution.py:35
  55.8 2.3 %copy.13 = bf16[2048,256]{1,0:T(8,128)(2,1)} copy(bf16[2048,256]{0,1:T(8,128)(2,1)} %fusion.3) | data formatting | bytes 2097152 | tf_op jit(solution)/shard_map/convert_element_type | solution.py:36
  (19 shorter events, 0.5 us)
Async XLA Ops:
  0.0 43.4 %copy-start = (bf16[1,8,3,256,256]{4,3,2,1,0:T(8,128)(2,1)S(1)}, bf16[1,8,3,256,256]{4,3,2,1,0:T(8,128)(2,1)}, u32[]{:S(2)}) copy-start(bf16[1,8,3,256,256]{4,3,2,1,0:T(8,128)(2,1)} %param.8) | copy-start | bytes 9437188
  14.6 7.0 %copy-start.1 = (s32[1,8,3]{1,0,2:T(1,128)S(1)}, s32[1,8,3]{1,0,2:T(1,128)}, u32[]{:S(2)}) copy-start(s32[1,8,3]{1,0,2:T(1,128)} %param.7) | copy-start | bytes 292
  14.7 1.7 %collective-permute-start.1 = (f32[256,256]{0,1:T(8,128)S(1)}, f32[256,256]{0,1:T(8,128)S(1)}, u32[]{:S(2)}, u32[]{:S(2)}) collective-permute-start(f32[256,256]{0,1:T(8,128)S(1)} %get-tuple-element.8), channel_id=1, source_target_pairs={{0,1},{1,0},{2,3},{3,2},{4,5},{5,4},{6,7},{7,6},{8,9},{9,8},{10,11... | collective-permute-start | bytes 786440 | tf_op jit(solution)/shard_map/ppermute | solution.py:14
  15.2 1.5 %collective-permute-start.6 = (f32[256,256]{0,1:T(8,128)S(1)}, f32[256,256]{0,1:T(8,128)S(1)}, u32[]{:S(2)}, u32[]{:S(2)}) collective-permute-start(f32[256,256]{0,1:T(8,128)S(1)} %get-tuple-element.9), channel_id=1, source_target_pairs={{0,1},{1,0},{2,3},{3,2},{4,5},{5,4},{6,7},{7,6},{8,9},{9,8},{10,11... | collective-permute-start | bytes 786440 | tf_op jit(solution)/shard_map/ppermute | solution.py:14
  15.3 1.8 %collective-permute-start.3 = (f32[256,256]{0,1:T(8,128)S(1)}, f32[256,256]{0,1:T(8,128)S(1)}, u32[]{:S(2)}, u32[]{:S(2)}) collective-permute-start(f32[256,256]{0,1:T(8,128)S(1)} %get-tuple-element.10), channel_id=1, source_target_pairs={{0,1},{1,0},{2,3},{3,2},{4,5},{5,4},{6,7},{7,6},{8,9},{9,8},{10,11... | collective-permute-start | bytes 786440 | tf_op jit(solution)/shard_map/ppermute | solution.py:14
  17.9 10.1 %collective-permute-start.7 = (f32[256,256]{0,1:T(8,128)S(1)}, f32[256,256]{0,1:T(8,128)}, u32[]{:S(2)}, u32[]{:S(2)}) collective-permute-start(f32[256,256]{0,1:T(8,128)S(1)} %get-tuple-element.6), channel_id=1, source_target_pairs={{0,2},{2,0},{1,3},{3,1},{4,6},{6,4},{5,7},{7,5},{8,10},{10,8},{9,1... | collective-permute-start | bytes 786440 | tf_op jit(solution)/shard_map/ppermute | solution.py:14
  21.4 29.1 %collective-permute-start = (bf16[256,256]{0,1:T(8,128)(2,1)}, bf16[256,256]{0,1:T(8,128)(2,1)}, u32[]{:S(2)}, u32[]{:S(2)}) collective-permute-start(bf16[256,256]{0,1:T(8,128)(2,1)} %fusion.12), channel_id=1, source_target_pairs={{0,1},{1,0},{2,3},{3,2},{4,5},{5,4},{6,7},{7,6},{8,9},{9,8},{10,11... | collective-permute-start | bytes 393224 | tf_op jit(solution)/shard_map/ppermute | solution.py:14
  21.4 15.6 %collective-permute-start.4 = (f32[256,256]{0,1:T(8,128)}, f32[256,256]{0,1:T(8,128)}, u32[]{:S(2)}, u32[]{:S(2)}) collective-permute-start(f32[256,256]{0,1:T(8,128)} %get-tuple-element.7), channel_id=1, source_target_pairs={{0,2},{2,0},{1,3},{3,1},{4,6},{6,4},{5,7},{7,5},{8,10},{10,8},{9,1... | collective-permute-start | bytes 786440 | tf_op jit(solution)/shard_map/ppermute | solution.py:14
  29.7 9.5 %collective-permute-start.8 = (f32[256,256]{0,1:T(8,128)}, f32[256,256]{0,1:T(8,128)S(1)}, u32[]{:S(2)}, u32[]{:S(2)}) collective-permute-start(f32[256,256]{0,1:T(8,128)} %add.51), channel_id=1, source_target_pairs={{0,4},{4,0},{1,5},{5,1},{2,6},{6,2},{3,7},{7,3},{8,12},{12,8},{9,1... | collective-permute-start | bytes 786440 | tf_op jit(solution)/shard_map/ppermute | solution.py:14
  35.5 15.0 %collective-permute-start.2 = (bf16[256,256]{0,1:T(8,128)(2,1)S(1)}, bf16[256,256]{0,1:T(8,128)(2,1)}, u32[]{:S(2)}, u32[]{:S(2)}) collective-permute-start(bf16[256,256]{0,1:T(8,128)(2,1)S(1)} %get-tuple-element.5), channel_id=1, source_target_pairs={{0,2},{2,0},{1,3},{3,1},{4,6},{6,4},{5,7},{7,5},{8,10},{10,8},{9,1... | collective-permute-start | bytes 393224 | tf_op jit(solution)/shard_map/ppermute | solution.py:14
  38.7 11.8 %collective-permute-start.5 = (bf16[256,256]{0,1:T(8,128)(2,1)}, bf16[256,256]{0,1:T(8,128)(2,1)}, u32[]{:S(2)}, u32[]{:S(2)}) collective-permute-start(bf16[256,256]{0,1:T(8,128)(2,1)} %add_convert_fusion.1), channel_id=1, source_target_pairs={{0,4},{4,0},{1,5},{5,1},{2,6},{6,2},{3,7},{7,3},{8,12},{12,8},{9,1... | collective-permute-start | bytes 393224 | tf_op jit(solution)/shard_map/ppermute | solution.py:14
  40.8 9.8 %collective-permute-start.9 = (bf16[256,256]{0,1:T(8,128)(2,1)}, bf16[256,256]{0,1:T(8,128)(2,1)S(1)}, u32[]{:S(2)}, u32[]{:S(2)}) collective-permute-start(bf16[256,256]{0,1:T(8,128)(2,1)} %add_convert_fusion), channel_id=1, source_target_pairs={{0,8},{8,0},{1,9},{9,1},{2,10},{10,2},{3,11},{11,3},{4,12},{12,4},... | collective-permute-start | bytes 393224 | tf_op jit(solution)/shard_map/ppermute | solution.py:14
where the time goes:
time: 58.4 us; the launch traced here: 58.1 us
  local copies, waits for them, and re-layouts  19.7 us (34%)
  matrix products  13.3 us (23%)
  starting transfers between devices  10.7 us (18%)
  waiting for transfers between devices  7.61 us (13%)
  other arithmetic  6.7 us (11%)
    ppermute x10, starting transfers between devices, from_partner(): return lax.ppermute(block, axis, route)  10.7 us
    gather x1, local copies, waits for them, and re-layouts, on_device(): ordered = features[vertex_order[0]]  9.95 us
    ppermute x10, waiting for transfers between devices, from_partner(): return lax.ppermute(block, axis, route)  7.61 us
    dot_general x1, matrix products, on_device(): jnp.einsum('bvr,brc->vc', basis, sibling, preferred_element_type=jnp.floa...  5.27 us
    dot_general x1, matrix products, on_device(): jnp.einsum('snij,snjc->sic', near_blocks[0], chosen, preferred_element_ty...  4.23 us
    convert_element_type x3, other arithmetic, on_device(): finished.append(from_partner(running.astype(jnp.bfloat16), 'leaf', level))  4.15 us
    dot_general x1, matrix products, on_device(): jnp.einsum('bvr,vc->brc', basis, ordered, preferred_element_type=jnp.floa...  3.77 us
    gather x1, local copies, waits for them, and re-layouts, on_device(): chosen = pieces[leaf_adjacency[0]]  3.71 us
  transfers between devices with their start and end apart: 10, of which 4 were waited for; matrix products, arithmetic and copies ran while one was open for 29% of the time, Pallas kernels for 0%

commit v1 on v0

v1 whole, which is shorter than its diff:
```python
import functools

import jax
import jax.numpy as jnp
from jax import lax
from jax.experimental import pallas as pl
from jax.experimental.pallas import tpu as pltpu
from jax.sharding import PartitionSpec as P

MESH = pl.DeviceIdType.MESH
F32 = jnp.float32
BF16 = jnp.bfloat16
MIN_CHUNK = 16
NT = (((1,), (1,)), ((), ()))


def group_bits(level, half):
    bits = level - 1
    while half >> bits < MIN_CHUNK:
        bits -= 1
    return bits


def plan(depth, half):
    ids, peers = {}, set()

    def add(key, distance):
        ids[key] = (len(ids), distance)
        peers.add(distance)

    for level in range(depth):
        if level == 0:
            add((0, "swap"), 1)
            continue
        bits = group_bits(level, half)
        add((level, "pair"), 1)
        for d in range(1, 1 << bits):
            add((level, "scatter", d), d << 1)
        for bit in range(bits + 1, level):
            add((level, "double", bit), 1 << bit)
        add((level, "swap"), 1 << level)
        for d in range(1, 1 << bits):
            add((level, "gather", d), d << 1)
        add((level, "share"), 1)
    return ids, sorted(peers)


def kernel(depth, order_ref, adj_ref, feat_hbm, near_hbm, basis_hbm, out_ref,
           feat, feat_t, ordered_t, near_v, basis_v, acc,
           proj, send, pair_in, half_out, group_in, own, chunk_out, double_in, sib,
           load_sem, send_sem, recv_sem):
    subs, nb, sub = near_v.shape[0], near_v.shape[1], near_v.shape[2]
    cols = feat.shape[1]
    half = cols // 2
    ids, peers = plan(depth, half)
    part = lax.axis_index("parts")
    me = lax.axis_index("leaf")
    core = lax.rem(me, 2)
    chip = me // 2

    def flip(index, distance):
        result = index
        bit = 0
        while distance >> bit:
            if distance >> bit & 1:
                result = result + (1 - 2 * lax.rem(index // (1 << bit), 2)) * (1 << bit)
            bit += 1
        return result

    def copy(key, src, dst):
        number, distance = ids[key]
        return pltpu.make_async_remote_copy(
            src_ref=src, dst_ref=dst, send_sem=send_sem.at[number], recv_sem=recv_sem.at[number],
            device_id=(part, flip(me, distance)), device_id_type=MESH)

    loads = [pltpu.make_async_copy(feat_hbm, feat, load_sem.at[0])]
    for level in reversed(range(depth)):
        loads.append(pltpu.make_async_copy(basis_hbm.at[level], basis_v.at[level], load_sem.at[1 + level]))
    loads.append(pltpu.make_async_copy(near_hbm.at[0], near_v, load_sem.at[1 + depth]))
    for load in loads:
        load.start()

    barrier = pltpu.get_barrier_semaphore()
    for distance in peers:
        pl.semaphore_signal(barrier, inc=1, device_id=(part, flip(me, distance)), device_id_type=MESH)

    loads[0].wait()
    for v in range(subs):
        feat_t[v] = feat[v * sub:(v + 1) * sub, :].T

    rows_in = lax.broadcasted_iota(jnp.int32, (sub, sub), 0)

    def pick(s, carry):
        wanted = order_ref[pl.ds(s, 1), :]
        total = jnp.zeros((cols, sub), F32)
        for v in range(subs):
            hot = jnp.where(rows_in == wanted - v * sub, 1.0, 0.0).astype(BF16)
            total = total + jnp.dot(feat_t[v], hot, preferred_element_type=F32)
        ordered_t[s] = total.astype(BF16)
        return carry

    lax.fori_loop(0, subs, pick, 0)

    pl.semaphore_wait(barrier, len(peers))
    started = {}

    def start(key, src, dst):
        started[key] = copy(key, src, dst)
        started[key].start()

    def mine(level):
        bits = group_bits(level, half)
        size = half >> bits
        member = lax.rem(chip, 1 << bits)
        return bits, size, member

    def far_rows(offset, size):
        return pl.ds(pl.multiple_of(offset, 16), size)

    for place, level in enumerate(reversed(range(depth))):
        loads[1 + place].wait()
        total = jnp.zeros((cols, basis_v.shape[2]), F32)
        for s in range(subs):
            total = total + jnp.dot(
                ordered_t[s], basis_v[level, s * sub:(s + 1) * sub, :], preferred_element_type=F32)
        send[level] = total.astype(BF16)
        if level == 0:
            start((0, "swap"), send.at[0], sib.at[0])
        else:
            proj[level] = total
            start((level, "pair"), send.at[level, far_rows((1 - core) * half, half)], pair_in.at[level])

    def after_pair(level):
        bits, size, member = mine(level)
        started[level, "pair"].wait_recv()
        total = proj[level, far_rows(core * half, half)] + pair_in[level].astype(F32)
        half_out[level] = total.astype(BF16)
        if bits == 0:
            return own_done(level, total, bits)
        own[level] = total
        for d in range(1, 1 << bits):
            other = flip(member, d)
            start((level, "scatter", d), half_out.at[level, far_rows(other * size, size)],
                  group_in.at[level, pl.ds((d - 1) * size, size)])

    def own_done(level, total, bits):
        size = half >> bits
        for bit in range(bits + 1, level):
            slot = bit - bits - 1
            chunk_out[level, slot, :size] = total.astype(BF16)
            start((level, "double", bit), chunk_out.at[level, slot, pl.ds(0, size)],
                  double_in.at[level, slot, pl.ds(0, size)])
            started[level, "double", bit].wait_recv()
            total = total + double_in[level, slot, :size].astype(F32)
        last = level - bits - 1
        chunk_out[level, last, :size] = total.astype(BF16)
        bits, size, member = mine(level)
        place = far_rows(core * half + member * size, size)
        start((level, "swap"), chunk_out.at[level, last, pl.ds(0, size)], sib.at[level, place])

    def after_scatter(level):
        bits, size, member = mine(level)
        if bits == 0:
            return
        total = own[level, far_rows(member * size, size)]
        for d in range(1, 1 << bits):
            started[level, "scatter", d].wait_recv()
            total = total + group_in[level, (d - 1) * size:d * size].astype(F32)
        own_done(level, total, bits)

    def after_swap(level):
        bits, size, member = mine(level)
        started[level, "swap"].wait_recv()
        place = far_rows(core * half + member * size, size)
        for d in range(1, 1 << bits):
            start((level, "gather", d), sib.at[level, place], sib.at[level, place])

    def gather_wait(level, d):
        bits, size, member = mine(level)
        place = far_rows(core * half + flip(member, d) * size, size)
        copy((level, "gather", d), sib.at[level, place], sib.at[level, place]).wait_recv()

    def after_gather(level):
        bits, size, member = mine(level)
        for d in range(1, 1 << bits):
            gather_wait(level, d)
        place = far_rows(core * half, half)
        start((level, "share"), sib.at[level, place], sib.at[level, place])

    def near_step(s, carry):
        total = jnp.zeros((sub, cols), F32)
        for k in range(nb):
            chosen = ordered_t[adj_ref[s * nb + k]]
            total = total + lax.dot_general(near_v[s, k], chosen, NT, preferred_element_type=F32)
        rows = pl.ds(pl.multiple_of(s * sub, sub), sub)
        acc[rows, :] = total
        return carry

    def far_step(levels, final):
        def body(s, carry):
            rows = pl.ds(pl.multiple_of(s * sub, sub), sub)
            total = acc[rows, :]
            for level in levels:
                total = total + lax.dot_general(
                    basis_v[level, rows, :], sib[level], NT, preferred_element_type=F32)
            if final:
                out_ref[rows, :] = total.astype(BF16)
            else:
                acc[rows, :] = total
            return carry

        lax.fori_loop(0, subs, body, 0)

    up = list(reversed(range(1, depth)))
    cut = [subs * i // 3 for i in range(4)]
    loads[1 + depth].wait()
    for level in up:
        after_pair(level)
    lax.fori_loop(cut[0], cut[1], near_step, 0)
    for level in up:
        after_scatter(level)
    lax.fori_loop(cut[1], cut[2], near_step, 0)
    for level in up:
        after_swap(level)
    lax.fori_loop(cut[2], cut[3], near_step, 0)
    for level in reversed(up):
        after_gather(level)
    started[0, "swap"].wait_recv()
    far_step([0], False)
    for level in reversed(up):
        place = far_rows((1 - core) * half, half)
        copy((level, "share"), sib.at[level, place], sib.at[level, place]).wait_recv()
    far_step(list(range(1, depth)), True)
    for key in started:
        started[key].wait_send()


def on_device(features, vertex_order, leaf_adjacency, near_blocks, basis):
    depth = lax.axis_size("leaf").bit_length() - 1
    leaf_rows, cols = features.shape
    _, subs, nb, sub, _ = near_blocks.shape
    rank = basis.shape[2]
    half = cols // 2
    count = len(plan(depth, half)[0])
    slots = max(level - group_bits(level, half) for level in range(1, depth))
    vmem = pl.BlockSpec(memory_space=pltpu.VMEM)
    hbm = pl.BlockSpec(memory_space=pl.ANY)
    return pl.pallas_call(
        functools.partial(kernel, depth),
        out_shape=jax.ShapeDtypeStruct((leaf_rows, cols), BF16),
        in_specs=[vmem, pl.BlockSpec(memory_space=pltpu.SMEM), hbm, hbm, hbm],
        out_specs=vmem,
        scratch_shapes=[
            pltpu.VMEM((leaf_rows, cols), BF16),
            pltpu.VMEM((subs, cols, sub), BF16),
            pltpu.VMEM((subs, cols, sub), BF16),
            pltpu.VMEM((subs, nb, sub, sub), BF16),
            pltpu.VMEM((depth, leaf_rows, rank), BF16),
            pltpu.VMEM((leaf_rows, cols), F32),
            pltpu.VMEM((depth, cols, rank), F32),
            pltpu.VMEM((depth, cols, rank), BF16),
            pltpu.VMEM((depth, half, rank), BF16),
            pltpu.VMEM((depth, half, rank), BF16),
            pltpu.VMEM((depth, half, rank), BF16),
            pltpu.VMEM((depth, half, rank), F32),
            pltpu.VMEM((depth, slots, half, rank), BF16),
            pltpu.VMEM((depth, slots, half, rank), BF16),
            pltpu.VMEM((depth, cols, rank), BF16),
            pltpu.SemaphoreType.DMA((2 + depth,)),
            pltpu.SemaphoreType.DMA((count,)),
            pltpu.SemaphoreType.DMA((count,)),
        ],
        compiler_params=pltpu.CompilerParams(
            collective_id=0, has_side_effects=True, vmem_limit_bytes=48 << 20),
    )(vertex_order.reshape(subs, sub), leaf_adjacency.reshape(subs * nb), features, near_blocks, basis)


def solution(mesh):
    placed = (
        P("leaf", "parts"),
        P("leaf", None),
        P("leaf", None, None),
        P("leaf", None, None, None, None),
        P(None, "leaf", None),
    )
    return jax.shard_map(
        on_device, mesh=mesh, in_specs=placed, out_specs=P("leaf", "parts"), check_vma=False
    )
```

time: 58.4 us -> 32.3 us (0.55)
  Pallas kernels: 0 us -> 25.3 us
  local copies, waits for them, and re-layouts: 19.7 us -> 5.43 us
  matrix products: 13.3 us -> 0 us
  starting transfers between devices: 10.7 us -> 0 us
  waiting for transfers between devices: 7.61 us -> 0 us
  other arithmetic: 6.7 us -> 1.36 us
    pallas_call x0 -> x1, Pallas kernels: none -> 25.3 us  [on_device(): pl.pallas_call(functools.partial(kernel, depth), out_shape=jax.ShapeDtype...]
    gather x2 -> x0, local copies, waits for them, and re-layouts: 13.7 us -> none  [the longest x1 9.95 us: on_device(): ordered = features[vertex_order[0]]]
    dot_general x3 -> x0, matrix products: 13.3 us -> none  [the longest x1 5.27 us: on_device(): jnp.einsum('bvr,brc->vc', basis, sibling, preferred_element_type=jnp.floa...]
    ppermute x10 -> x0, starting transfers between devices: 10.7 us -> none  [from_partner(): return lax.ppermute(block, axis, route)]
    ppermute x10 -> x0, waiting for transfers between devices: 7.61 us -> none  [from_partner(): return lax.ppermute(block, axis, route)]
    unnamed x4 -> x7, local copies, waits for them, and re-layouts: 0.01 us -> 5.35 us
    convert_element_type x3 -> x0, other arithmetic: 4.15 us -> none  [on_device(): finished.append(from_partner(running.astype(jnp.bfloat16), 'leaf', level))]
    convert_element_type x2 -> x0, local copies, waits for them, and re-layouts: 2.92 us -> none  [the longest x1 2.26 us: on_device(): return (near + far).astype(jnp.bfloat16)]
  transfers between devices with their start and end apart: 10 -> 0, of which waited for: 4 -> 0; matrix products, arithmetic and copies ran while one was open for 29% -> 0% of each run, Pallas kernels for 0% -> 0%
where the time goes in v1:
time: 32.3 us; the launch traced here: 32.1 us
  Pallas kernels  25.3 us (78%)
  local copies, waits for them, and re-layouts  5.43 us (17%)
  other arithmetic  1.36 us (4%)
    pallas_call x1, Pallas kernels, on_device(): pl.pallas_call(functools.partial(kernel, depth), out_shape=jax.ShapeDtype...  25.3 us
    unnamed x7, local copies, waits for them, and re-layouts  5.35 us
    unnamed x1, other arithmetic  1.36 us

profile of v1, /device:TPU:0, one launch (start us, length us, event | category | flops | bytes accessed | tf_op | source)
XLA Modules:
  0.0 32.1 jit_solution(14845930828290906114)
XLA Ops:
  0.0 0.8 %copy.7 = s32[1,8,3]{2,1,0:T(8,128)S(1)} copy(s32[1,8,3]{1,0,2:T(1,128)} %param.7) | data formatting | bytes 192 | tf_op args[2]
  0.8 0.1 reshape.7.adj_ref
  0.8 0.5 %broadcast.3 = s32[]{:T(128)} broadcast(s32[]{:T(128)} %constant.6), dimensions={} | broadcast | bytes 8 | tf_op args[1]
  1.4 1.4 %reduce.3 = s32[2048]{0:T(1024)S(1)} reduce(s32[1,2048]{1,0:T(1,128)} %param.6, s32[]{:T(128)} %broadcast.3), dimensions={0}, to_apply=%param.6.reduce_sub_computation.3 | reduce | bytes 16388 | tf_op args[1]
  2.7 0.0 copy-start
  2.7 1.9 %copy-done = bf16[1,8,3,256,256]{4,3,2,1,0:T(8,128)(2,1)S(1)} copy-done((bf16[1,8,3,256,256]{4,3,2,1,0:T(8,128)(2,1)S(1)}, bf16[1,8,3,256,256]{4,3,2,1,0:T(8,128)(2,1)}, u32[]{:S(2)}) %copy-start) | copy-done | bytes 3145752
  4.6 0.0 copy-start.1
  4.6 1.2 %copy-done.1 = bf16[2048,256]{1,0:T(8,128)(2,1)S(1)} copy-done((bf16[2048,256]{1,0:T(8,128)(2,1)S(1)}, bf16[2048,256]{1,0:T(8,128)(2,1)}, u32[]{:S(2)}) %copy-start.1) | copy-done | bytes 1048600
  5.8 25.3 %shard_map.55 = bf16[2048,256]{1,0:T(8,128)(2,1)S(1)} custom-call(s32[8,256]{1,0:T(8,128)S(1)} %reshape.6.order_ref, s32[24]{0:T(128)S(1)} %reshape.7.adj_ref, bf16[2048,256]{1,0:T(8,128)(2,1)S(1)} %copy-done.1, bf16[1,8,3,256,256]{4,3,2,1,0:T(8,128)(2,1)S(1)} %copy-done, bf16[4,2048,256]{2,1,0:T(8,128)(2,1)} %basis_hbm.1), custom_call_target="tpu_custom_call" | custom-call | tf_op jit(solution)/shard_map/pallas_call | solution.py:248
  31.1 1.0 %copy.9 = bf16[2048,256]{1,0:T(8,128)(2,1)} copy(bf16[2048,256]{1,0:T(8,128)(2,1)S(1)} %shard_map.55) | data formatting | bytes 2097152
  (1 shorter events, 0.0 us)
Async XLA Ops:
  2.7 1.9 %copy-start = (bf16[1,8,3,256,256]{4,3,2,1,0:T(8,128)(2,1)S(1)}, bf16[1,8,3,256,256]{4,3,2,1,0:T(8,128)(2,1)}, u32[]{:S(2)}) copy-start(bf16[1,8,3,256,256]{4,3,2,1,0:T(8,128)(2,1)} %near_hbm.1) | copy-start | bytes 9437188
  4.6 1.2 %copy-start.1 = (bf16[2048,256]{1,0:T(8,128)(2,1)S(1)}, bf16[2048,256]{1,0:T(8,128)(2,1)}, u32[]{:S(2)}) copy-start(bf16[2048,256]{1,0:T(8,128)(2,1)} %feat_hbm.1) | copy-start | bytes 3145732

commit v2 on v1

--- a/solution.py
+++ b/solution.py
@@ -11,7 +11,6 @@
 F32 = jnp.float32
 BF16 = jnp.bfloat16
 MIN_CHUNK = 16
-NT = (((1,), (1,)), ((), ()))
 
 
 def group_bits(level, half):
@@ -38,17 +37,16 @@
             add((level, "scatter", d), d << 1)
         for bit in range(bits + 1, level):
             add((level, "double", bit), 1 << bit)
-        add((level, "swap"), 1 << level)
-        for d in range(1, 1 << bits):
-            add((level, "gather", d), d << 1)
+        for d in range(1 << bits):
+            add((level, "swap", d), (1 << level) + (d << 1))
         add((level, "share"), 1)
     return ids, sorted(peers)
 
 
-def kernel(depth, order_ref, adj_ref, feat_hbm, near_hbm, basis_hbm, out_ref,
-           feat, feat_t, ordered_t, near_v, basis_v, acc,
-           proj, send, pair_in, half_out, group_in, own, chunk_out, double_in, sib,
-           load_sem, send_sem, recv_sem):
+def kernel(depth, order_hbm, adj_hbm, feat_hbm, near_hbm, basis_hbm, out_ref,
+           feat, feat_t, ordered_t, ordered, near_v, basis_v, acc,
+           proj, send, pair_in, half_out, group_in, own, chunk_out, double_in, sib, sib_t,
+           order_ref, adj_ref, load_sem, send_sem, recv_sem):
     subs, nb, sub = near_v.shape[0], near_v.shape[1], near_v.shape[2]
     cols = feat.shape[1]
     half = cols // 2
@@ -77,6 +75,9 @@
     for level in reversed(range(depth)):
         loads.append(pltpu.make_async_copy(basis_hbm.at[level], basis_v.at[level], load_sem.at[1 + level]))
     loads.append(pltpu.make_async_copy(near_hbm.at[0], near_v, load_sem.at[1 + depth]))
+    loads.append(pltpu.make_async_copy(adj_hbm, adj_ref, load_sem.at[2 + depth]))
+    order_load = pltpu.make_async_copy(order_hbm, order_ref, load_sem.at[3 + depth])
+    order_load.start()
     for load in loads:
         load.start()
 
@@ -85,21 +86,23 @@
         pl.semaphore_signal(barrier, inc=1, device_id=(part, flip(me, distance)), device_id_type=MESH)
 
     loads[0].wait()
+    order_load.wait()
     for v in range(subs):
         feat_t[v] = feat[v * sub:(v + 1) * sub, :].T
 
     rows_in = lax.broadcasted_iota(jnp.int32, (sub, sub), 0)
 
     def pick(s, carry):
-        wanted = order_ref[pl.ds(s, 1), :]
+        wanted = order_ref[:, pl.ds(pl.multiple_of(s * sub, sub), sub)]
         total = jnp.zeros((cols, sub), F32)
         for v in range(subs):
             hot = jnp.where(rows_in == wanted - v * sub, 1.0, 0.0).astype(BF16)
             total = total + jnp.dot(feat_t[v], hot, preferred_element_type=F32)
         ordered_t[s] = total.astype(BF16)
+        ordered[s] = total.astype(BF16).T
         return carry
 
-    lax.fori_loop(0, subs, pick, 0)
+    lax.fori_loop(0, subs, pick, 0, unroll=True)
 
     pl.semaphore_wait(barrier, len(peers))
     started = {}
@@ -117,8 +120,8 @@
     def far_rows(offset, size):
         return pl.ds(pl.multiple_of(offset, 16), size)
 
-    for place, level in enumerate(reversed(range(depth))):
-        loads[1 + place].wait()
+    def project(level):
+        loads[depth - level].wait()
         total = jnp.zeros((cols, basis_v.shape[2]), F32)
         for s in range(subs):
             total = total + jnp.dot(
@@ -156,7 +159,8 @@
         chunk_out[level, last, :size] = total.astype(BF16)
         bits, size, member = mine(level)
         place = far_rows(core * half + member * size, size)
-        start((level, "swap"), chunk_out.at[level, last, pl.ds(0, size)], sib.at[level, place])
+        for d in range(1 << bits):
+            start((level, "swap", d), chunk_out.at[level, last, pl.ds(0, size)], sib.at[level, place])
 
     def after_scatter(level):
         bits, size, member = mine(level)
@@ -170,67 +174,68 @@
 
     def after_swap(level):
         bits, size, member = mine(level)
-        started[level, "swap"].wait_recv()
-        place = far_rows(core * half + member * size, size)
-        for d in range(1, 1 << bits):
-            start((level, "gather", d), sib.at[level, place], sib.at[level, place])
-
-    def gather_wait(level, d):
-        bits, size, member = mine(level)
-        place = far_rows(core * half + flip(member, d) * size, size)
-        copy((level, "gather", d), sib.at[level, place], sib.at[level, place]).wait_recv()
-
-    def after_gather(level):
-        bits, size, member = mine(level)
-        for d in range(1, 1 << bits):
-            gather_wait(level, d)
+        for d in range(1 << bits):
+            place = far_rows(core * half + flip(member, d) * size, size)
+            copy((level, "swap", d), sib.at[level, place], sib.at[level, place]).wait_recv()
         place = far_rows(core * half, half)
         start((level, "share"), sib.at[level, place], sib.at[level, place])
+
+    def after_share(level):
+        if level == 0:
+            started[0, "swap"].wait_recv()
+        else:
+            place = far_rows((1 - core) * half, half)
+            copy((level, "share"), sib.at[level, place], sib.at[level, place]).wait_recv()
+        sib_t[level] = sib[level].T
 
     def near_step(s, carry):
         total = jnp.zeros((sub, cols), F32)
         for k in range(nb):
-            chosen = ordered_t[adj_ref[s * nb + k]]
-            total = total + lax.dot_general(near_v[s, k], chosen, NT, preferred_element_type=F32)
+            chosen = ordered[adj_ref[k, 0, s]]
+            total = total + jnp.dot(near_v[s, k], chosen, preferred_element_type=F32)
         rows = pl.ds(pl.multiple_of(s * sub, sub), sub)
         acc[rows, :] = total
         return carry
 
+    tall = subs * sub
+
     def far_step(levels, final):
         def body(s, carry):
-            rows = pl.ds(pl.multiple_of(s * sub, sub), sub)
+            rows = pl.ds(pl.multiple_of(s * tall, tall), tall)
             total = acc[rows, :]
             for level in levels:
-                total = total + lax.dot_general(
-                    basis_v[level, rows, :], sib[level], NT, preferred_element_type=F32)
+                total = total + jnp.dot(
+                    basis_v[level, rows, :], sib_t[level], preferred_element_type=F32)
             if final:
                 out_ref[rows, :] = total.astype(BF16)
             else:
                 acc[rows, :] = total
             return carry
 
-        lax.fori_loop(0, subs, body, 0)
+        lax.fori_loop(0, subs * sub // tall, body, 0)
 
     up = list(reversed(range(1, depth)))
-    cut = [subs * i // 3 for i in range(4)]
+    for place, level in enumerate(reversed(range(depth))):
+        project(level)
+        if place >= 2:
+            after_pair(up[place - 2])
+    for level in up[max(depth - 2, 0):]:
+        after_pair(level)
     loads[1 + depth].wait()
-    for level in up:
-        after_pair(level)
-    lax.fori_loop(cut[0], cut[1], near_step, 0)
+    loads[2 + depth].wait()
+    lax.fori_loop(0, subs, near_step, 0, unroll=True)
     for level in up:
         after_scatter(level)
-    lax.fori_loop(cut[1], cut[2], near_step, 0)
-    for level in up:
+    after_share(0)
+    far_step([0], False)
+    after_swap(1)
+    after_share(1)
+    far_step([1], False)
+    for level in reversed(up[:-1]):
         after_swap(level)
-    lax.fori_loop(cut[2], cut[3], near_step, 0)
-    for level in reversed(up):
-        after_gather(level)
-    started[0, "swap"].wait_recv()
-    far_step([0], False)
-    for level in reversed(up):
-        place = far_rows((1 - core) * half, half)
-        copy((level, "share"), sib.at[level, place], sib.at[level, place]).wait_recv()
-    far_step(list(range(1, depth)), True)
+    for level in range(2, depth):
+        after_share(level)
+        far_step([level], level == depth - 1)
     for key in started:
         started[key].wait_send()
 
@@ -244,16 +249,17 @@
     count = len(plan(depth, half)[0])
     slots = max(level - group_bits(level, half) for level in range(1, depth))
     vmem = pl.BlockSpec(memory_space=pltpu.VMEM)
-    hbm = pl.BlockSpec(memory_space=pl.ANY)
+    hbm = pl.BlockSpec(memory_space=pltpu.HBM)
     return pl.pallas_call(
         functools.partial(kernel, depth),
         out_shape=jax.ShapeDtypeStruct((leaf_rows, cols), BF16),
-        in_specs=[vmem, pl.BlockSpec(memory_space=pltpu.SMEM), hbm, hbm, hbm],
+        in_specs=[hbm] * 5,
         out_specs=vmem,
         scratch_shapes=[
             pltpu.VMEM((leaf_rows, cols), BF16),
             pltpu.VMEM((subs, cols, sub), BF16),
             pltpu.VMEM((subs, cols, sub), BF16),
+            pltpu.VMEM((subs, sub, cols), BF16),
             pltpu.VMEM((subs, nb, sub, sub), BF16),
             pltpu.VMEM((depth, leaf_rows, rank), BF16),
             pltpu.VMEM((leaf_rows, cols), F32),
@@ -266,13 +272,16 @@
             pltpu.VMEM((depth, slots, half, rank), BF16),
             pltpu.VMEM((depth, slots, half, rank), BF16),
             pltpu.VMEM((depth, cols, rank), BF16),
-            pltpu.SemaphoreType.DMA((2 + depth,)),
+            pltpu.VMEM((depth, rank, cols), BF16),
+            pltpu.VMEM((1, leaf_rows), jnp.int32),
+            pltpu.SMEM((nb, 1, subs), jnp.int32),
+            pltpu.SemaphoreType.DMA((4 + depth,)),
             pltpu.SemaphoreType.DMA((count,)),
             pltpu.SemaphoreType.DMA((count,)),
         ],
         compiler_params=pltpu.CompilerParams(
-            collective_id=0, has_side_effects=True, vmem_limit_bytes=48 << 20),
-    )(vertex_order.reshape(subs, sub), leaf_adjacency.reshape(subs * nb), features, near_blocks, basis)
+            collective_id=0, has_side_effects=True, vmem_limit_bytes=64 << 20),
+    )(vertex_order, jnp.transpose(leaf_adjacency, (2, 0, 1)), features, near_blocks, basis)
 
 
 def solution(mesh):

time: 32.3 us -> 22.5 us (0.70)
  Pallas kernels: 25.3 us -> 19.9 us
  local copies, waits for them, and re-layouts: 5.43 us -> 2.26 us
  other arithmetic: 1.36 us -> 0 us
    pallas_call x1, Pallas kernels: 25.3 us -> 19.9 us  [on_device(): pl.pallas_call(functools.partial(kernel, depth), out_shape=jax.ShapeDtype...]
    unnamed x7 -> x1, local copies, waits for them, and re-layouts: 5.35 us -> 2.26 us
    unnamed x1 -> x0, other arithmetic: 1.36 us -> none
where the time goes in v2:
time: 22.5 us; the launch traced here: 22.2 us
  Pallas kernels  19.9 us (88%)
  local copies, waits for them, and re-layouts  2.26 us (10%)
    pallas_call x1, Pallas kernels, on_device(): pl.pallas_call(functools.partial(kernel, depth), out_shape=jax.ShapeDtype...  19.9 us
    unnamed x1, local copies, waits for them, and re-layouts  2.26 us

profile of v2, /device:TPU:0, one launch (start us, length us, event | category | flops | bytes accessed | tf_op | source)
XLA Modules:
  0.0 22.2 jit_solution(5939128571473647835)
XLA Ops:
  0.0 19.9 %shard_map.55 = bf16[2048,256]{1,0:T(8,128)(2,1)} custom-call(s32[1,2048]{1,0:T(1,128)} %order_hbm.1, s32[3,1,8]{2,1,0:T(1,128)} %bitcast.1, bf16[2048,256]{1,0:T(8,128)(2,1)} %feat_hbm.1, bf16[1,8,3,256,256]{4,3,2,1,0:T(8,128)(2,1)} %near_hbm.1, bf16[4,2048,256]{2,1,0:T(8,128)(2,1)} %basis_hbm.1), custom_call_target="tpu_custom_call" | custom-call | tf_op jit(solution)/shard_map/pallas_call | solution.py:253
  19.9 2.3 %copy.7 = bf16[2048,256]{1,0:T(8,128)(2,1)} copy(bf16[2048,256]{1,0:T(8,128)(2,1)} %shard_map.55) | data formatting | bytes 2097152

commit v3 on v2

--- a/solution.py
+++ b/solution.py
@@ -280,8 +280,8 @@
             pltpu.SemaphoreType.DMA((count,)),
         ],
         compiler_params=pltpu.CompilerParams(
-            collective_id=0, has_side_effects=True, vmem_limit_bytes=64 << 20),
-    )(vertex_order, jnp.transpose(leaf_adjacency, (2, 0, 1)), features, near_blocks, basis)
+            collective_id=0, has_side_effects=True, vmem_limit_bytes=52 << 20),
+    )(*[pltpu.with_memory_space_constraint(x, pltpu.HBM) for x in (vertex_order, jnp.transpose(leaf_adjacency, (2, 0, 1)), features, near_blocks, basis)])
 
 
 def solution(mesh):

time: 22.5 us -> 20.2 us (0.90)
  local copies, waits for them, and re-layouts: 2.26 us -> 0.97 us
  Pallas kernels: 19.9 us -> 18.9 us
    unnamed x1, local copies, waits for them, and re-layouts: 2.26 us -> 0.97 us
    pallas_call x1, Pallas kernels: 19.9 us -> 18.9 us  [on_device(): pl.pallas_call(functools.partial(kernel, depth), out_shape=jax.ShapeDtype...]
where the time goes in v3:
time: 20.2 us; the launch traced here: 19.9 us
  Pallas kernels  18.9 us (94%)
  local copies, waits for them, and re-layouts  0.97 us (5%)
    pallas_call x1, Pallas kernels, on_device(): pl.pallas_call(functools.partial(kernel, depth), out_shape=jax.ShapeDtype...  18.9 us
    unnamed x1, local copies, waits for them, and re-layouts  0.97 us

profile of v3, /device:TPU:0, one launch (start us, length us, event | category | flops | bytes accessed | tf_op | source)
XLA Modules:
  0.0 19.9 jit_solution(17828487495181679264)
XLA Ops:
  0.0 18.9 %shard_map.55 = bf16[2048,256]{1,0:T(8,128)(2,1)S(1)} custom-call(s32[1,2048]{1,0:T(1,128)} %order_hbm.1, s32[3,1,8]{2,1,0:T(1,128)} %bitcast.1, bf16[2048,256]{1,0:T(8,128)(2,1)} %feat_hbm.1, bf16[1,8,3,256,256]{4,3,2,1,0:T(8,128)(2,1)} %near_hbm.1, bf16[4,2048,256]{2,1,0:T(8,128)(2,1)} %basis_hbm.1), custom_call_target="tpu_custom_call" | custom-call | tf_op jit(solution)/shard_map/pallas_call | solution.py:253
  18.9 1.0 %copy.7 = bf16[2048,256]{1,0:T(8,128)(2,1)} copy(bf16[2048,256]{1,0:T(8,128)(2,1)S(1)} %shard_map.55) | data formatting | bytes 2097152

commit v4 on v3

--- a/solution.py
+++ b/solution.py
@@ -78,8 +78,7 @@
     loads.append(pltpu.make_async_copy(adj_hbm, adj_ref, load_sem.at[2 + depth]))
     order_load = pltpu.make_async_copy(order_hbm, order_ref, load_sem.at[3 + depth])
     order_load.start()
-    for load in loads:
-        load.start()
+    loads[0].start()
 
     barrier = pltpu.get_barrier_semaphore()
     for distance in peers:
@@ -87,6 +86,8 @@
 
     loads[0].wait()
     order_load.wait()
+    for load in loads[1:]:
+        load.start()
     for v in range(subs):
         feat_t[v] = feat[v * sub:(v + 1) * sub, :].T
 
@@ -99,7 +100,6 @@
             hot = jnp.where(rows_in == wanted - v * sub, 1.0, 0.0).astype(BF16)
             total = total + jnp.dot(feat_t[v], hot, preferred_element_type=F32)
         ordered_t[s] = total.astype(BF16)
-        ordered[s] = total.astype(BF16).T
         return carry
 
     lax.fori_loop(0, subs, pick, 0, unroll=True)
@@ -223,6 +223,8 @@
         after_pair(level)
     loads[1 + depth].wait()
     loads[2 + depth].wait()
+    for s in range(subs):
+        ordered[s] = ordered_t[s].T
     lax.fori_loop(0, subs, near_step, 0, unroll=True)
     for level in up:
         after_scatter(level)

time: 20.2 us -> 20.5 us (1.015)
  Pallas kernels: 18.9 us -> 19.2 us
    pallas_call x1, Pallas kernels: 18.9 us -> 19.2 us  [on_device(): pl.pallas_call(functools.partial(kernel, depth), out_shape=jax.ShapeDtype...]
where the time goes in v4:
time: 20.5 us; the launch traced here: 20.2 us
  Pallas kernels  19.2 us (94%)
  local copies, waits for them, and re-layouts  0.97 us (5%)
    pallas_call x1, Pallas kernels, on_device(): pl.pallas_call(functools.partial(kernel, depth), out_shape=jax.ShapeDtype...  19.2 us
    unnamed x1, local copies, waits for them, and re-layouts  0.97 us

profile of v4, /device:TPU:0, one launch (start us, length us, event | category | flops | bytes accessed | tf_op | source)
XLA Modules:
  0.0 20.2 jit_solution(12594032304043100723)
XLA Ops:
  0.0 19.2 %shard_map.55 = bf16[2048,256]{1,0:T(8,128)(2,1)S(1)} custom-call(s32[1,2048]{1,0:T(1,128)} %order_hbm.1, s32[3,1,8]{2,1,0:T(1,128)} %bitcast.1, bf16[2048,256]{1,0:T(8,128)(2,1)} %feat_hbm.1, bf16[1,8,3,256,256]{4,3,2,1,0:T(8,128)(2,1)} %near_hbm.1, bf16[4,2048,256]{2,1,0:T(8,128)(2,1)} %basis_hbm.1), custom_call_target="tpu_custom_call" | custom-call | tf_op jit(solution)/shard_map/pallas_call | solution.py:255
  19.2 1.0 %copy.7 = bf16[2048,256]{1,0:T(8,128)(2,1)} copy(bf16[2048,256]{1,0:T(8,128)(2,1)S(1)} %shard_map.55) | data formatting | bytes 2097152
